TPU v7x, 32 devices: a whole 2x2x4 slice. The times are simulated.
32 devices in a mesh: row: 8 (over z, y), col: 4 (over x, core).
Axes of the slice: x: 2, y: 2, z: 4, core: 2. Of those that a mesh axis runs over, the one named last changes fastest.
Arguments:
- tensor: bfloat16 [2048, 8192], P(('row', 'col')), may hold values from -6 to 6
- density: bfloat16 [2, 4096, 8192], P(None, 'col', 'row'), may hold values from -0.125 to 0.125
- tensor_mask: int32 [16, 64], replicated, may hold values 0 or 1
- density_mask: int32 [64, 64], replicated, may hold values 0 or 1
- pair_rows: int32 [32], replicated, may hold values from 0 to 31, as said below
Outputs:
- contracted: bfloat16 [2048, 8192], P(('row', 'col'))
Inputs may be any that keep to these rules, and one draw needn't show every extreme that they name: pair_rows is a permutation of 0 to 31. Among the 8 slots that share one remainder modulo 4, at most 3 hold units of any one group of 8 consecutive units, and for every remainder some group gets exactly 3.
All inputs are finite; a program needn't handle non-finite values.
Results may differ from a plain program's by a relative error of at most 0.001.
Values may be sent and summed in bfloat16 or wider, within the bound.
A program may use at most 64 MiB of HBM per device.

v0:
```python
import jax
import jax.numpy as jnp
from jax import lax
from jax.sharding import PartitionSpec as P

BLOCK = 128


def on_device(tensor, density, tensor_mask, density_mask, pair_rows):
    row_count = lax.axis_size("row")
    col_count = lax.axis_size("col")
    row_index = lax.axis_index("row")
    col_index = lax.axis_index("col")
    unit_rows, orbitals = tensor.shape
    owner_slot = row_index * col_count + col_index
    own_unit = pair_rows[owner_slot]
    mask_rows = (own_unit * unit_rows + jnp.arange(unit_rows, dtype=jnp.int32)) // BLOCK
    row_mask = jnp.repeat(
        jnp.take(tensor_mask, mask_rows, axis=0).astype(jnp.bfloat16), BLOCK, axis=1
    )
    masked = tensor * row_mask
    piece_rows = density.shape[1]
    piece_width = density.shape[2]
    half_rows = orbitals // 2
    global_rows = (
        jnp.arange(2)[:, None] * half_rows
        + col_index * piece_rows
        + jnp.arange(piece_rows)[None, :]
    )
    global_cols = row_index * piece_width + jnp.arange(piece_width)
    dens_mask = jnp.take(
        jnp.take(density_mask, (global_rows // BLOCK).reshape(-1), axis=0),
        global_cols // BLOCK,
        axis=1,
    )
    density_pair = density * dens_mask.reshape(2, piece_rows, piece_width).astype(jnp.bfloat16)
    column = lax.all_gather(density_pair, "col", axis=1, tiled=True).reshape(orbitals, piece_width)
    tile_result = jnp.dot(
        lax.all_gather(masked, "row", axis=0, tiled=True),
        column,
        preferred_element_type=jnp.float32,
    ).astype(jnp.bfloat16)
    tile_result = tile_result.reshape(row_count, unit_rows, piece_width)
    owned_rows = lax.all_to_all(tile_result, "row", split_axis=0, concat_axis=2, tiled=True)
    return owned_rows.reshape(unit_rows, orbitals)


def solution(mesh):
    placed = (P(("row", "col"), None), P(None, "col", "row"), P(), P(), P())
    return jax.shard_map(
        on_device, mesh=mesh, in_specs=placed, out_specs=P(("row", "col"), None), check_vma=False
    )
```

profile of v0, /device:TPU:0, one launch (start us, length us, event | category | flops | bytes accessed | tf_op | source)
XLA Modules:
  0.0 300.5 jit_solution(1032798503816356706)
XLA Ops:
  6.5 0.0 copy-start
  6.5 0.0 all-gather.3.cloned.1.call-start
  6.5 1.2 dynamic_slice.3
  8.5 1.3 gather_fusion
  9.8 0.1 select_convert_fusion.1
  9.9 0.6 broadcast_in_dim.37
  10.5 2.9 bitcast_multiply_fusion
  13.4 0.0 all-gather.3.cloned.1.call-update
  13.4 0.0 all-gather.5.cloned.1.call-start
  13.5 0.1 fusion.4
  13.6 0.0 copy-done
  13.6 5.5 %gather_fusion.1 = s32[2048,64]{1,0:T(8,128)S(1)} fusion(s32[64,64]{1,0:T(8,128)S(1)} %copy-done, s32[2048]{0:T(1024)S(1)} %broadcast_clamp_fusion), kind=kCustom, calls=%fused_computation.1 | custom fusion | bytes 1056768 | tf_op jit(solution)/shard_map/jit(_take)/gather | solution.py:32
  19.1 0.3 broadcast_select_fusion
  19.5 0.3 copy.9
  19.8 6.8 %gather_fusion.2 = s32[1024,2048]{1,0:T(8,128)} fusion(s32[2048,64]{0,1:T(8,128)S(1)} %copy.9, s32[1024]{0:T(1024)S(1)} %broadcast_clamp_fusion.1), kind=kCustom, calls=%fused_computation.2 | custom fusion | bytes 16781312 | tf_op jit(solution)/shard_map/jit(_take)/gather | solution.py:31
  26.7 9.3 %copy.12 = s32[2048,1024]{1,0:T(8,128)} copy(s32[2048,1024]{0,1:T(8,128)} %bitcast.47) | data formatting | bytes 16777216 | tf_op jit(solution)/shard_map/jit(_take)/gather | solution.py:31
  36.0 8.3 %fusion = bf16[2,1024,1024]{2,1,0:T(8,128)(2,1)} fusion(bf16[2,1024,1024]{2,1,0:T(8,128)(2,1)} %param.6, s32[2,1024,1024]{2,1,0:T(8,128)} %bitcast.48, pred[1024]{0:T(1024)(128)(4,1)S(1)} %compare_and_fusion.1), kind=kLoop, calls=%fused_computation.4 | loop fusion | flops 6291456 | bytes 16778240 | tf_op jit(solution)/shard_map/mul | solution.py:36
  44.3 0.0 all-gather.5.cloned.1.call-update
  44.3 96.4 %all-gather.3.cloned.1.call-done = bf16[512,8192]{1,0:T(8,128)(2,1)} async-done(((bf16[64,8192]{1,0:T(8,128)(2,1)}), bf16[512,8192]{1,0:T(8,128)(2,1)}) %all-gather.3.cloned.1.call-update) | async-done | bytes 8388624 | tf_op jit(solution)/shard_map/all_gather | solution.py:39
  140.7 105.7 %all-gather.5.cloned.1.call-done = bf16[2,4096,1024]{2,1,0:T(8,128)(2,1)} async-done(((bf16[2,1024,1024]{2,1,0:T(8,128)(2,1)}), bf16[2,4096,1024]{2,1,0:T(8,128)(2,1)}) %all-gather.5.cloned.1.call-update) | async-done | bytes 16777232 | tf_op jit(solution)/shard_map/all_gather | solution.py:37
  246.4 14.8 %convolution_convert_fusion = bf16[512,1024]{1,0:T(8,128)(2,1)S(1)} fusion(bf16[512,8192]{1,0:T(8,128)(2,1)} %all-gather.3.cloned.1.call-done, bf16[8192,1024]{1,0:T(8,128)(2,1)} %bitcast.55), kind=kOutput, calls=%fused_computation.5 | convolution fusion | flops 8590458880 | bytes 26214400 | tf_op jit(solution)/shard_map/dot_general | solution.py:38
  261.2 31.4 %all_to_all.15 = bf16[8,64,1024]{2,1,0:T(8,128)(2,1)S(1)} all-to-all(bf16[8,64,1024]{2,1,0:T(8,128)(2,1)S(1)} %bitcast.51), channel_id=1, replica_groups=mesh['row'=8,'col'=4] {'row'}, dimensions={0} | all-to-all | bytes 2097152 | tf_op jit(solution)/shard_map/all_to_all | solution.py:44
  292.6 1.1 copy.16
  (11 shorter events, 0.2 us)
Async XLA Ops:
  6.5 7.1 %copy-start = (s32[64,64]{1,0:T(8,128)S(1)}, s32[64,64]{1,0:T(8,128)}, u32[]{:S(2)}) copy-start(s32[64,64]{1,0:T(8,128)} %param.8) | copy-start | bytes 49156
  6.5 134.2 %all-gather.3.cloned.1.call-start = ((), (), s32[]{:S(2)}) async-start(), calls=%async_computation.1 | async-start | bytes 9437184 | tf_op jit(solution)/shard_map/all_gather | solution.py:39
  13.4 233.0 %all-gather.5.cloned.1.call-start = ((), (), s32[]{:S(2)}) async-start(), calls=%async_computation.2 | async-start | bytes 20971520 | tf_op jit(solution)/shard_map/all_gather | solution.py:37
Sparse Core Ops, SparseCore 0:
  13.5 127.1 all-gather.2
  142.3 104.0 all-gather.4
where the time goes:
time: 301 us
  waiting for transfers between devices  202 us (67%)
  blocking collectives  31.4 us (10%)
  local copies, waits for them, and re-layouts  26.1 us (9%)
  matrix products  14.8 us (5%)
  between operations  14.2 us (5%)
  other arithmetic  11.8 us (4%)
    all_gather x1, waiting for transfers between devices, on_device(): lax.all_gather(density_pair, 'col', axis=1, tiled=True)  106 us
    all_gather x1, waiting for transfers between devices, on_device(): lax.all_gather(masked, 'row', axis=0, tiled=True)  96.4 us
    all_to_all x1, blocking collectives, on_device(): lax.all_to_all(tile_result, 'row', split_axis=0, concat_axis=2, tiled=True)  31.4 us
    gather x2, local copies, waits for them, and re-layouts, on_device(): jnp.take(jnp.take(density_mask, (global_rows // BLOCK).reshape(-1), axis=...  16.1 us
    dot_general x1, matrix products, on_device(): jnp.dot(lax.all_gather(masked, 'row', axis=0, tiled=True), column, prefer...  14.8 us
    mul x1, other arithmetic, on_device(): density * dens_mask.reshape(2, piece_rows, piece_width).astype(jnp.bfloat16)  8.29 us
  transfers between devices with their start and end apart: 2, of which 2 were waited for; matrix products, arithmetic and copies ran while one was open for 10% of the time, Pallas kernels for 0%

commit v1 on v0

--- a/solution.py
+++ b/solution.py
@@ -2,6 +2,7 @@
 import jax.numpy as jnp
 from jax import lax
 from jax.sharding import PartitionSpec as P
+from jax.lax import all_gather
 
 BLOCK = 128
 
@@ -34,7 +35,13 @@
         axis=1,
     )
     density_pair = density * dens_mask.reshape(2, piece_rows, piece_width).astype(jnp.bfloat16)
-    column = lax.all_gather(density_pair, "col", axis=1, tiled=True).reshape(orbitals, piece_width)
+
+    def ratios_unite(unit, axis_name="col"):
+        w_next = all_gather(unit, axis_name)
+        prior = jnp.concatenate(w_next, 1)
+        return prior
+
+    column = ratios_unite(density_pair).reshape(orbitals, piece_width)
     tile_result = jnp.dot(
         lax.all_gather(masked, "row", axis=0, tiled=True),
         column,

time: 301 us -> 325 us (1.080)
  waiting for transfers between devices: 202 us -> 217 us
  local copies, waits for them, and re-layouts: 26.1 us -> 39.3 us
    all_gather x1, waiting for transfers between devices: 96.4 us -> 113 us  [on_device(): lax.all_gather(masked, 'row', axis=0, tiled=True)]
    reshape x0 -> x1, local copies, waits for them, and re-layouts: none -> 14 us  [ratios_unite(): prior = jnp.concatenate(w_next, 1)]
  transfers between devices with their start and end apart: 2 -> 2, of which waited for: 2 -> 2; matrix products, arithmetic and copies ran while one was open for 10% -> 5% of each run, Pallas kernels for 0% -> 0%
where the time goes in v1:
time: 325 us; the launch traced here: 324 us
  waiting for transfers between devices  217 us (67%)
  local copies, waits for them, and re-layouts  39.3 us (12%)
  blocking collectives  28.3 us (9%)
  matrix products  14.8 us (5%)
  between operations  14.2 us (4%)
  other arithmetic  10.6 us (3%)
    all_gather x1, waiting for transfers between devices, on_device(): lax.all_gather(masked, 'row', axis=0, tiled=True)  113 us
    all_gather x1, waiting for transfers between devices, ratios_unite(): w_next = all_gather(unit, axis_name)  104 us
    all_to_all x1, blocking collectives, on_device(): lax.all_to_all(tile_result, 'row', split_axis=0, concat_axis=2, tiled=True)  28.3 us
    gather x2, local copies, waits for them, and re-layouts, on_device(): jnp.take(jnp.take(density_mask, (global_rows // BLOCK).reshape(-1), axis=...  16.1 us
    dot_general x1, matrix products, on_device(): jnp.dot(lax.all_gather(masked, 'row', axis=0, tiled=True), column, prefer...  14.8 us
    reshape x1, local copies, waits for them, and re-layouts, ratios_unite(): prior = jnp.concatenate(w_next, 1)  14 us
    mul x1, other arithmetic, on_device(): density * dens_mask.reshape(2, piece_rows, piece_width).astype(jnp.bfloat16)  8.28 us
  transfers between devices with their start and end apart: 2, of which 2 were waited for; matrix products, arithmetic and copies ran while one was open for 5% of the time, Pallas kernels for 0%

profile of v1, /device:TPU:0, one launch (start us, length us, event | category | flops | bytes accessed | tf_op | source)
XLA Modules:
  0.0 324.3 jit_solution(9262958949079658965)
XLA Ops:
  6.5 0.0 copy-start
  6.5 0.0 all-gather.6.cloned.1.call-start
  6.6 0.1 fusion.4
  6.8 0.5 copy-done
  7.3 5.5 %gather_fusion.1 = s32[2048,64]{1,0:T(8,128)S(1)} fusion(s32[64,64]{1,0:T(8,128)S(1)} %copy-done, s32[2048]{0:T(1024)S(1)} %broadcast_clamp_fusion), kind=kCustom, calls=%fused_computation.1 | custom fusion | bytes 1056768 | tf_op jit(solution)/shard_map/jit(_take)/gather | solution.py:33
  12.8 0.3 broadcast_select_fusion
  13.1 0.3 copy.16
  13.4 6.9 %gather_fusion.2 = s32[1024,2048]{1,0:T(8,128)} fusion(s32[2048,64]{0,1:T(8,128)S(1)} %copy.16, s32[1024]{0:T(1024)S(1)} %broadcast_clamp_fusion.1), kind=kCustom, calls=%fused_computation.2 | custom fusion | bytes 16781312 | tf_op jit(solution)/shard_map/jit(_take)/gather | solution.py:32
  20.3 9.3 %copy.20 = s32[2048,1024]{1,0:T(8,128)} copy(s32[2048,1024]{0,1:T(8,128)} %bitcast.50) | data formatting | bytes 16777216 | tf_op jit(solution)/shard_map/jit(_take)/gather | solution.py:32
  29.6 0.0 copy-start.4
  29.6 0.0 copy-start.2
  29.6 0.0 copy-start.3
  29.6 8.3 %fusion = bf16[2,1024,1024]{2,1,0:T(8,128)(2,1)} fusion(bf16[2,1024,1024]{2,1,0:T(8,128)(2,1)} %param.6, s32[2,1024,1024]{2,1,0:T(8,128)} %bitcast.51, pred[1024]{0:T(1024)(128)(4,1)S(1)} %compare_and_fusion.1), kind=kLoop, calls=%fused_computation.4 | loop fusion | flops 6291456 | bytes 16778240 | tf_op jit(solution)/shard_map/mul | solution.py:37
  37.8 0.0 all-gather.6.cloned.1.call-update
  37.9 0.0 all-gather.4.cloned.1.call-start
  37.9 0.0 copy-done.4
  37.9 0.6 dynamic_slice.3
  39.2 0.0 copy-done.2
  39.2 0.6 gather_fusion
  39.8 0.1 select_convert_fusion.1
  39.9 0.6 broadcast_in_dim.37
  40.5 0.0 copy-done.3
  40.5 1.7 bitcast_multiply_fusion
  42.2 0.0 all-gather.4.cloned.1.call-update
  42.2 104.4 %all-gather.6.cloned.1.call-done = bf16[8,1024,1024]{2,1,0:T(8,128)(2,1)} async-done(((bf16[2,1024,1024]{2,1,0:T(8,128)(2,1)}), bf16[8,1024,1024]{2,1,0:T(8,128)(2,1)}) %all-gather.6.cloned.1.call-update) | async-done | bytes 16777232 | tf_op jit(solution)/shard_map/all_gather | solution.py:40
  146.6 14.0 %copy.18 = bf16[2,4,1024,1024]{3,2,1,0:T(8,128)(2,1)} copy(bf16[2,4,1024,1024]{3,2,0,1:T(8,128)(2,1)} %bitcast.52) | data formatting | bytes 33554432 | tf_op jit(solution)/shard_map/reshape | solution.py:41
  160.7 112.6 %all-gather.4.cloned.1.call-done = bf16[512,8192]{1,0:T(8,128)(2,1)} async-done(((bf16[64,8192]{1,0:T(8,128)(2,1)}), bf16[512,8192]{1,0:T(8,128)(2,1)}) %all-gather.4.cloned.1.call-update) | async-done | bytes 8388624 | tf_op jit(solution)/shard_map/all_gather | solution.py:46
  273.3 0.0 copy-start.1
  273.3 14.8 %convolution_convert_fusion = bf16[512,1024]{1,0:T(8,128)(2,1)S(1)} fusion(bf16[512,8192]{1,0:T(8,128)(2,1)} %all-gather.4.cloned.1.call-done, bf16[8192,1024]{1,0:T(8,128)(2,1)} %bitcast.53), kind=kOutput, calls=%fused_computation.5 | convolution fusion | flops 8590458880 | bytes 26214400 | tf_op jit(solution)/shard_map/dot_general | solution.py:45
  288.1 28.3 %all_to_all.15 = bf16[8,64,1024]{2,1,0:T(8,128)(2,1)S(1)} all-to-all(bf16[8,64,1024]{2,1,0:T(8,128)(2,1)S(1)} %bitcast.56), channel_id=1, replica_groups=mesh['row'=8,'col'=4] {'row'}, dimensions={0} | all-to-all | bytes 2097152 | tf_op jit(solution)/shard_map/all_to_all | solution.py:51
  316.4 1.1 copy.24
  317.5 0.0 copy-done.1
  (11 shorter events, 0.2 us)
Async XLA Ops:
  6.5 0.8 copy-start
  6.5 140.1 %all-gather.6.cloned.1.call-start = ((), (), s32[]{:S(2)}) async-start(), calls=%async_computation.2 | async-start | bytes 20971520 | tf_op jit(solution)/shard_map/all_gather | solution.py:40
  29.6 8.4 %copy-start.4 = (s32[32]{0:T(128)S(1)}, s32[32]{0:T(128)}, u32[]{:S(2)}) copy-start(s32[32]{0:T(128)} %param.9) | copy-start | bytes 388
  29.6 9.6 %copy-start.2 = (s32[16,64]{1,0:T(8,128)S(1)}, s32[16,64]{1,0:T(8,128)}, u32[]{:S(2)}) copy-start(s32[16,64]{1,0:T(8,128)} %param.7) | copy-start | bytes 12292
  29.6 11.0 %copy-start.3 = (bf16[64,8192]{1,0:T(8,128)(2,1)S(1)}, bf16[64,8192]{1,0:T(8,128)(2,1)}, u32[]{:S(2)}) copy-start(bf16[64,8192]{1,0:T(8,128)(2,1)} %param.5) | copy-start | bytes 3145732
  37.9 235.4 %all-gather.4.cloned.1.call-start = ((), (), s32[]{:S(2)}) async-start(), calls=%async_computation.1 | async-start | bytes 9437184 | tf_op jit(solution)/shard_map/all_gather | solution.py:46
  273.3 44.2 %copy-start.1 = (s32[64,64]{1,0:T(8,128)S(1)}, s32[64,64]{1,0:T(8,128)}, u32[]{:S(2)}) copy-start(s32[64,64]{1,0:T(8,128)} %param.8) | copy-start | bytes 49156
Sparse Core Ops, SparseCore 0:
  38.0 108.6 all-gather.5
  148.8 124.4 all-gather.3
